TPU v7x, 32 devices: a whole 2x2x4 slice. The times are simulated.
32 devices in a mesh: frame: 4 (over y, x), head: 8 (over z, core).
Axes of the slice: x: 2, y: 2, z: 4, core: 2. Of those that a mesh axis runs over, the one named last changes fastest.
Arguments:
- tokens: bfloat16 [4096, 5120], P('frame', 'head'), may hold values from -16 to 16
- qkv_weight: bfloat16 [3, 5120, 2048], P(None, None, 'head'), may hold values from -0.1118034 to 0.1118034
- out_weight: bfloat16 [2048, 5120], P('head'), may hold values from -0.1875 to 0.1875
- modulation: float32 [3, 5120], replicated, may hold values from -3 to 3
- block_mask: int32 [16, 32, 32], P('head', 'frame'), may hold values from 0 to 1, as said below
Outputs:
- mixed: bfloat16 [4096, 5120], P('frame', 'head')
Inputs may be any that keep to these rules, and one draw needn't show every extreme that they name: `block_mask`: 1 keeps a pair of 128-token blocks; every query block keeps its own block.
All inputs are finite; a program needn't handle non-finite values.
Results may differ from a plain program's by a relative error of at most 0.0085.
Values may be sent and summed in bfloat16 or wider, within the bound.
A program may use at most 256 MiB of HBM per device.

v0:
```python
import functools
import math

import jax
import jax.numpy as jnp
from jax import lax
from jax.experimental import pallas as pl
from jax.experimental.pallas import tpu as pltpu
from jax.sharding import PartitionSpec as P

BLK = 128
NEGATIVE = -1e30
EPSILON = 1e-06
LOG2E = math.log2(math.e)
TOKEN_CHUNKS = 8
QUERY_CHUNKS = 8


def source_of(me, size, step):
    if size & (size - 1) == 0:
        return lax.bitwise_xor(me, step)
    return lax.rem(me + size - step, size)


def target_of(me, size, step):
    if size & (size - 1) == 0:
        return lax.bitwise_xor(me, step)
    return lax.rem(me + step, size)


def chain(me, size):
    return me // 2, me % 2, me + 1 - 2 * (me % 2)


def send(src, dst, send_sem, recv_sem, **where):
    return pltpu.make_async_remote_copy(
        src_ref=src,
        dst_ref=dst,
        send_sem=send_sem,
        recv_sem=recv_sem,
        device_id=where,
        device_id_type=pl.DeviceIdType.MESH,
    )


class Relay:
    def __init__(self, me, size, buffer, span, sems):
        self.me, self.size, self.buffer, self.span = me, size, buffer, span
        self.spot, self.core, self.other = chain(me, size)
        self.line = size // 2
        self.far_send, self.far_recv, self.pair_send, self.pair_recv = sems

    def rows(self, block, chunk):
        start = pl.multiple_of(chunk * self.span, self.span)
        return self.buffer.at[block, pl.ds(start, self.span), :]

    def hop(self, block, chunk, away, source=None):
        ref = self.rows(block, chunk)
        slot = 0 if away > 0 else 1
        return send(
            ref if source is None else source,
            ref,
            self.far_send.at[block // 2, chunk, slot],
            self.far_recv.at[block // 2, chunk],
            head=self.me + 2 * away,
        )

    def pair(self, block, chunk, source=None):
        ref = self.rows(block, chunk)
        return send(
            ref if source is None else source,
            ref,
            self.pair_send.at[block // 2, chunk],
            self.pair_recv.at[block // 2, chunk],
            head=self.other,
        )

    def own(self, chunk, source=None):
        for away in (1, -1):
            edge = self.spot < self.line - 1 if away > 0 else self.spot > 0

            @pl.when(edge)
            def _():
                self.hop(self.me, chunk, away, source).start()

        self.pair(self.me, chunk, source).start()

    def pass_on(self, chunk, distance):
        for away in (1, -1):
            spot = self.spot - away * distance
            here = spot >= 0 if away > 0 else spot < self.line
            edge = self.spot < self.line - 1 if away > 0 else self.spot > 0
            block = spot * 2 + self.core

            @pl.when(here)
            def _():
                self.hop(block, chunk, away).wait_recv()

                @pl.when(edge)
                def _():
                    self.hop(block, chunk, away).start()

                self.pair(block, chunk).start()

    def advance(self, turn, count):
        for distance in range(1, self.line):
            chunk = turn - (distance - 1)

            @pl.when(jnp.logical_and(chunk >= 0, chunk < count))
            def _():
                self.pass_on(chunk, distance)

    def collect(self, chunk):
        for spot in range(self.line):
            self.pair(spot * 2 + 1 - self.core, chunk).wait_recv()

    def drain(self, chunk):
        for spot in range(self.line):
            block = spot * 2 + self.core
            self.pair(block, chunk).wait_send()
            for away in (1, -1):
                came = spot <= self.spot if away > 0 else spot >= self.spot
                edge = self.spot < self.line - 1 if away > 0 else self.spot > 0

                @pl.when(jnp.logical_and(came, edge))
                def _():
                    self.hop(block, chunk, away).wait_send()


def greet(me, frame, heads_axis, frames):
    barrier = pltpu.get_barrier_semaphore()
    for s in range(1, frames):
        pl.semaphore_signal(
            barrier, inc=1, device_id={"frame": target_of(frame, frames, s)},
            device_id_type=pl.DeviceIdType.MESH,
        )
    for s in range(1, heads_axis):
        pl.semaphore_signal(
            barrier, inc=1, device_id={"head": target_of(me, heads_axis, s)},
            device_id_type=pl.DeviceIdType.MESH,
        )
    pl.semaphore_wait(barrier, frames + heads_axis - 2)


def contract(parts, weight):
    cols = parts[0].shape[1]
    if cols % 128 == 0:
        return jnp.dot(
            jnp.concatenate(parts, axis=1), weight, preferred_element_type=jnp.float32
        )
    total = 0.0
    for i, part in enumerate(parts):
        total += jnp.dot(
            part, weight[i * cols : (i + 1) * cols], preferred_element_type=jnp.float32
        )
    return total


def gather_kernel(
    frames, heads_axis, count, w_slice, tokens, modulation, weight, out_weight, q_ref, kv_ref,
    band_ref, got, held, far_send, far_recv, pair_send, pair_recv, kv_send, kv_recv, w_send,
    w_recv, local,
):
    me, frame = lax.axis_index("head"), lax.axis_index("frame")
    rows, cols = tokens.shape
    span = rows // count
    inner = q_ref.shape[1]
    width = cols * heads_axis
    load = pltpu.make_async_copy(weight, held, local.at[0])
    load.start()
    mine = pltpu.make_async_copy(tokens, got.at[me], local.at[1])
    mine.start()
    share = band_ref.shape[1]
    band = pl.ds(pl.multiple_of(frame * share, share), share)
    keep = pltpu.make_async_copy(w_slice(out_weight, band, me), band_ref.at[me], local.at[2])
    keep.start()
    greet(me, frame, heads_axis, frames)
    relay = Relay(me, heads_axis, got, span, (far_send, far_recv, pair_send, pair_recv))

    def begin(chunk, carry):
        start = pl.multiple_of(chunk * span, span)
        relay.own(chunk, tokens.at[pl.ds(start, span), :])
        return carry

    lax.fori_loop(0, count, begin, 0)
    mine.wait()
    load.wait()

    def to_frame(chunk, s):
        start = pl.multiple_of(chunk * span, span)
        return send(
            kv_ref.at[0, :, pl.ds(start, span), :],
            kv_ref.at[s, :, pl.ds(start, span), :],
            kv_send.at[chunk, s],
            kv_recv.at[chunk, s],
            frame=target_of(frame, frames, s),
        )

    def to_head(s):
        there = target_of(me, heads_axis, s)
        return send(
            w_slice(out_weight, band, there), band_ref.at[me], w_send.at[s], w_recv.at[s],
            head=there,
        )

    late = max(heads_axis // 2 - 2, 0)

    def turn(i, carry):
        relay.advance(i, count)

        @pl.when(i == count + late - 2)
        def _():
            for s in range(1, heads_axis):
                to_head(s).start()

        @pl.when(i >= late)
        def _():
            step(i - late)

        return carry

    def step(chunk):
        relay.collect(chunk)
        start = pl.multiple_of(chunk * span, span)
        window = pl.ds(start, span)
        total = jnp.zeros((span, cols), jnp.float32)
        for i in range(heads_axis):
            total += got[i, window, :].astype(jnp.float32)
        center = jnp.sum(total, axis=1, keepdims=True) / width
        square = jnp.zeros((span, cols), jnp.float32)
        for i in range(heads_axis):
            off = got[i, window, :].astype(jnp.float32) - center
            square += off * off
        inverse = lax.rsqrt(jnp.sum(square, axis=1, keepdims=True) / width + EPSILON)
        parts = []
        for i in range(heads_axis):
            wide = got[i, window, :].astype(jnp.float32)
            shift = modulation[0:1, i * cols : (i + 1) * cols]
            gain = modulation[1:2, i * cols : (i + 1) * cols]
            parts.append(
                ((wide - center) * inverse * (1.0 + gain) + shift).astype(jnp.bfloat16)
            )
        sums = [contract(parts, held[j]) for j in range(3)]
        q_ref[window, :] = sums[0].astype(q_ref.dtype)
        kv_ref[0, 0, window, :] = sums[1].astype(kv_ref.dtype)
        kv_ref[0, 1, window, :] = sums[2].astype(kv_ref.dtype)
        for s in range(1, frames):
            to_frame(chunk, s).start()

    lax.fori_loop(0, count + late, turn, 0)

    def finish(chunk, carry):
        relay.drain(chunk)
        for s in range(1, frames):
            to_frame(chunk, s).wait()
        return carry

    lax.fori_loop(0, count, finish, 0)
    keep.wait()
    for s in range(1, heads_axis):
        there = source_of(me, heads_axis, s)
        ref = band_ref.at[there]
        send(ref, ref, w_send.at[s], w_recv.at[s], head=target_of(me, heads_axis, s)).wait_recv()
        to_head(s).wait_send()


def gather_project(frames, heads_axis, tokens, modulation, weight, out_weight):
    rows, cols = tokens.shape
    inner = weight.shape[2]
    count = TOKEN_CHUNKS
    line = heads_axis // 2
    whole = pl.BlockSpec(memory_space=pltpu.VMEM)
    away = pl.BlockSpec(memory_space=pl.ANY)
    sem = pltpu.SemaphoreType.DMA
    if cols % 128 == 0:
        def w_slice(ref, band, there):
            return ref.at[band, pl.ds(pl.multiple_of(there * cols, cols), cols)]
    else:
        out_weight = out_weight.reshape(inner, heads_axis, cols).transpose(1, 0, 2)

        def w_slice(ref, band, there):
            return ref.at[there, band, :]

    return pl.pallas_call(
        functools.partial(gather_kernel, frames, heads_axis, count, w_slice),
        in_specs=[away, whole, away, away],
        out_specs=[whole, whole, whole],
        out_shape=[
            jax.ShapeDtypeStruct((rows, inner), jnp.bfloat16),
            jax.ShapeDtypeStruct((frames, 2, rows, inner), jnp.bfloat16),
            jax.ShapeDtypeStruct((heads_axis, inner // frames, cols), jnp.bfloat16),
        ],
        scratch_shapes=[
            pltpu.VMEM((heads_axis, rows, cols), jnp.bfloat16),
            pltpu.VMEM(weight.shape, jnp.bfloat16),
            sem((line, count, 2)),
            sem((line, count)),
            sem((line, count)),
            sem((line, count)),
            sem((count, frames)),
            sem((count, frames)),
            sem((heads_axis,)),
            sem((heads_axis,)),
            sem((3,)),
        ],
        compiler_params=pltpu.CompilerParams(collective_id=0, has_side_effects=True),
        name="gather_project",
    )(tokens, modulation, weight, out_weight)


def attend_kernel(
    frames, heads_axis, heads, count, q_ref, kv_ref, mask_ref, band_ref, tokens, gate,
    out_ref, done, full, far_send, far_recv, pair_send, pair_recv, x_send, x_recv, local,
):
    me, frame = lax.axis_index("head"), lax.axis_index("frame")
    rows, inner = q_ref.shape
    head_size = inner // heads
    factor = LOG2E / math.sqrt(head_size)
    span = rows // count
    share = inner // frames
    greet(me, frame, heads_axis, frames)
    relay = Relay(me, heads_axis, done, span, (far_send, far_recv, pair_send, pair_recv))
    band = pl.ds(pl.multiple_of(frame * share, share), share)

    keep = pltpu.make_async_copy(band_ref, full.at[:, band, :], local.at[0])
    keep.start()

    def to_frame(s):
        return send(
            band_ref, full.at[:, band, :], x_send.at[s], x_recv.at[s],
            frame=target_of(frame, frames, s),
        )

    def from_frame(s):
        there = source_of(frame, frames, s)
        part = pl.ds(pl.multiple_of(there * share, share), share)
        return send(
            full.at[:, part, :], full.at[:, part, :], x_send.at[s], x_recv.at[s],
            frame=target_of(frame, frames, s),
        )

    for s in range(1, frames):
        to_frame(s).start()
    sources = [source_of(frame, frames, s) * (rows // BLK) for s in range(frames)]

    wide = span // BLK

    def tile(t, carry):
        window = pl.ds(pl.multiple_of(t * span, span), span)
        for h in range(heads):
            lanes = slice(h * head_size, (h + 1) * head_size)
            query = q_ref[window, lanes]
            top = jnp.full((1, span), NEGATIVE, jnp.float32)
            total = jnp.zeros((1, span), jnp.float32)
            summed = jnp.zeros((head_size, span), jnp.float32)
            for slot in range(frames):
                scores = lax.dot_general(
                    kv_ref[slot, 0, :, lanes], query, (((1,), (1,)), ((), ())),
                    preferred_element_type=jnp.float32,
                )
                pieces = []
                new_top = top
                for block in range(rows // BLK):
                    row = jnp.concatenate(
                        [
                            jnp.full(
                                (1, BLK),
                                jnp.where(
                                    mask_ref[h, t * wide + k, sources[slot] + block] > 0,
                                    0.0,
                                    NEGATIVE,
                                ),
                                jnp.float32,
                            )
                            for k in range(wide)
                        ],
                        axis=1,
                    )
                    part = scores[block * BLK : (block + 1) * BLK] * factor + row
                    new_top = jnp.maximum(new_top, jnp.max(part, axis=0, keepdims=True))
                    pieces.append(part)
                fade = jnp.exp2(top - new_top)
                total = total * fade
                weights = [jnp.exp2(p - new_top) for p in pieces]
                for w in weights:
                    total += jnp.sum(w, axis=0, keepdims=True)
                joined = jnp.concatenate([w.astype(jnp.bfloat16) for w in weights], axis=0)
                summed = summed * fade + lax.dot_general(
                    kv_ref[slot, 1, :, lanes], joined, (((0,), (0,)), ((), ())),
                    preferred_element_type=jnp.float32,
                )
                top = new_top
            done[me, window, lanes] = (summed / total).T.astype(done.dtype)

        relay.own(t)

        @pl.when(t >= 1)
        def _():
            relay.advance(t - 1, count)

        return carry

    lax.fori_loop(0, count, tile, 0)

    late = max(heads_axis // 2 - 2, 0)

    def rest(i, carry):
        relay.advance(i, count)
        return carry

    lax.fori_loop(count - 1, count + late - 1, rest, 0)
    keep.wait()
    for s in range(1, frames):
        from_frame(s).wait_recv()

    def out(t, carry):
        @pl.when(t == count - 1)
        def _():
            relay.advance(count + late - 1, count)

        relay.collect(t)
        window = pl.ds(pl.multiple_of(t * span, span), span)
        weight = full[...].reshape(heads_axis * inner, full.shape[2])
        total = contract([done[i, window, :] for i in range(heads_axis)], weight)
        if gate.shape[1] == out_ref.shape[1]:
            own = gate[...]
        else:
            cols = out_ref.shape[1]
            own = gate[2:3, pl.ds(pl.multiple_of(me * cols, cols), cols)]
        held = tokens[window, :].astype(jnp.float32)
        out_ref[window, :] = (held + own * total).astype(out_ref.dtype)
        return carry

    lax.fori_loop(0, count, out, 0)

    def finish(t, carry):
        relay.drain(t)
        return carry

    lax.fori_loop(0, count, finish, 0)
    for s in range(1, frames):
        to_frame(s).wait_send()


def attend_mix(frames, heads_axis, heads, query, pairs, mask, band, tokens, gate):
    rows, inner = query.shape
    cols = tokens.shape[1]
    count = QUERY_CHUNKS
    line = heads_axis // 2
    whole = pl.BlockSpec(memory_space=pltpu.VMEM)
    away = pl.BlockSpec(memory_space=pl.ANY)
    sem = pltpu.SemaphoreType.DMA
    return pl.pallas_call(
        functools.partial(attend_kernel, frames, heads_axis, heads, count),
        in_specs=[whole, whole, pl.BlockSpec(memory_space=pltpu.SMEM), whole, whole, whole],
        out_specs=whole,
        out_shape=jax.ShapeDtypeStruct((rows, cols), jnp.bfloat16),
        scratch_shapes=[
            pltpu.VMEM((heads_axis, rows, inner), jnp.bfloat16),
            pltpu.VMEM((heads_axis, inner, cols), jnp.bfloat16),
            sem((line, count, 2)),
            sem((line, count)),
            sem((line, count)),
            sem((line, count)),
            sem((frames,)),
            sem((frames,)),
            sem((1,)),
        ],
        compiler_params=pltpu.CompilerParams(collective_id=1, has_side_effects=True),
        name="attend_mix",
    )(query, pairs, mask, band, tokens, gate)


def shards(frames, heads_axis, tokens, qkv_weight, out_weight, modulation, block_mask):
    local_rows, local_cols = tokens.shape
    heads_here = block_mask.shape[0]
    head = lax.axis_index("head")
    gate = modulation
    if local_cols % 128:
        gate = lax.dynamic_slice_in_dim(modulation[2:3], head * local_cols, local_cols, 1)

    query, pairs, band = gather_project(
        frames, heads_axis, tokens, modulation, qkv_weight, out_weight
    )
    return attend_mix(frames, heads_axis, heads_here, query, pairs, block_mask, band, tokens, gate)


def solution(mesh):
    placed = (
        P("frame", "head"),
        P(None, None, "head"),
        P("head", None),
        P(),
        P("head", "frame", None),
    )
    body = functools.partial(shards, mesh.shape["frame"], mesh.shape["head"])
    return jax.shard_map(
        body, mesh=mesh, in_specs=placed, out_specs=P("frame", "head"), check_vma=False
    )
```

profile of v0, /device:TPU:1, one launch (start us, length us, event | category | flops | bytes accessed | tf_op | source)
XLA Modules:
  0.0 167.2 jit_solution(15706429761399980481)
XLA Ops:
  0.0 113.5 %gather_project.1 = (bf16[1024,256]{1,0:T(8,128)(2,1)}, bf16[4,2,1024,256]{3,2,1,0:T(8,128)(2,1)}, bf16[8,64,640]{2,1,0:T(8,128)(2,1)}) custom-call(bf16[1024,640]{1,0:T(8,128)(2,1)} %tokens.3, f32[3,5120]{1,0:T(4,128)} %gate.1, bf16[3,5120,256]{2,1,0:T(8,128)(2,1)} %weight.1, bf16[256,5120]{1,0:T(8,128)(2,1)} %out_weight.1), custom_call_target="tpu_custom_call" | custom-call | tf_op jit(solution)/shard_map/gather_project/pallas_call | solution.py:284
  113.5 51.3 %attend_mix.1 = bf16[1024,640]{1,0:T(8,128)(2,1)} custom-call(bf16[1024,256]{1,0:T(8,128)(2,1)} %get-tuple-element.8.q_ref, bf16[4,2,1024,256]{3,2,1,0:T(8,128)(2,1)} %get-tuple-element.9.kv_ref, s32[2,8,32]{2,1,0:T(8,128)} %mask_ref.1, bf16[8,64,640]{2,1,0:T(8,128)(2,1)} %get-tuple-element.10.band_ref, bf16[1024,640]{1,0:T(8,128)(2,1)} %tokens.3, ...), custom_call_target="tpu_custom_call" | custom-call | tf_op jit(solution)/shard_map/attend_mix/pallas_call | solution.py:453
  164.8 2.5 %copy.7 = bf16[1024,640]{1,0:T(8,128)(2,1)} copy(bf16[1024,640]{1,0:T(8,128)(2,1)} %attend_mix.1) | data formatting | bytes 2621440
where the time goes:
time: 167 us
  Pallas kernels  165 us (99%)
  local copies, waits for them, and re-layouts  2.49 us (1%)
    pallas_call x1, Pallas kernels, gather_project(): pl.pallas_call(functools.partial(gather_kernel, frames, heads_axis, count...  113 us
    pallas_call x1, Pallas kernels, attend_mix(): pl.pallas_call(functools.partial(attend_kernel, frames, heads_axis, heads...  51.3 us

commit v1 on v0

--- a/solution.py
+++ b/solution.py
@@ -12,8 +12,7 @@
 NEGATIVE = -1e30
 EPSILON = 1e-06
 LOG2E = math.log2(math.e)
-TOKEN_CHUNKS = 8
-QUERY_CHUNKS = 8
+CHUNKS = 8
 
 
 def source_of(me, size, step):
@@ -85,12 +84,15 @@
 
         self.pair(self.me, chunk, source).start()
 
-    def pass_on(self, chunk, distance):
+    def pass_on(self, chunk, distance, ends=None):
         for away in (1, -1):
             spot = self.spot - away * distance
             here = spot >= 0 if away > 0 else spot < self.line
             edge = self.spot < self.line - 1 if away > 0 else self.spot > 0
             block = spot * 2 + self.core
+            if ends is not None:
+                far = 0 if away > 0 else self.line - 1
+                here = spot == far if ends else jnp.logical_and(here, spot != far)
 
             @pl.when(here)
             def _():
@@ -109,6 +111,10 @@
             @pl.when(jnp.logical_and(chunk >= 0, chunk < count))
             def _():
                 self.pass_on(chunk, distance)
+
+    def pass_all(self, chunk, ends):
+        for distance in range(1, self.line):
+            self.pass_on(chunk, distance, ends)
 
     def collect(self, chunk):
         for spot in range(self.line):
@@ -156,30 +162,41 @@
     return total
 
 
-def gather_kernel(
-    frames, heads_axis, count, w_slice, tokens, modulation, weight, out_weight, q_ref, kv_ref,
-    band_ref, got, held, far_send, far_recv, pair_send, pair_recv, kv_send, kv_recv, w_send,
-    w_recv, local,
+def block_kernel(
+    frames, heads_axis, heads, count, w_slice, tokens, modulation, weight, out_weight, mask_ref,
+    gate, out_ref, got, held, q_ref, kv_ref, band_ref, full, done,
+    t_far_send, t_far_recv, t_pair_send, t_pair_recv,
+    h_far_send, h_far_recv, h_pair_send, h_pair_recv,
+    kv_send, kv_recv, w_send, w_recv, x_send, x_recv, local,
 ):
     me, frame = lax.axis_index("head"), lax.axis_index("frame")
     rows, cols = tokens.shape
     span = rows // count
     inner = q_ref.shape[1]
     width = cols * heads_axis
+    line = heads_axis // 2
+    share = band_ref.shape[1]
+    head_size = inner // heads
+    factor = LOG2E / math.sqrt(head_size)
+    wide = span // BLK
+    inside = jnp.logical_and(me // 2 > 0, me // 2 < line - 1)
+
     load = pltpu.make_async_copy(weight, held, local.at[0])
     load.start()
     mine = pltpu.make_async_copy(tokens, got.at[me], local.at[1])
     mine.start()
-    share = band_ref.shape[1]
     band = pl.ds(pl.multiple_of(frame * share, share), share)
     keep = pltpu.make_async_copy(w_slice(out_weight, band, me), band_ref.at[me], local.at[2])
     keep.start()
     greet(me, frame, heads_axis, frames)
-    relay = Relay(me, heads_axis, got, span, (far_send, far_recv, pair_send, pair_recv))
+    relay = Relay(me, heads_axis, got, span, (t_far_send, t_far_recv, t_pair_send, t_pair_recv))
+    spread = Relay(me, heads_axis, done, span, (h_far_send, h_far_recv, h_pair_send, h_pair_recv))
+
+    def rows_of(chunk):
+        return pl.ds(pl.multiple_of(chunk * span, span), span)
 
     def begin(chunk, carry):
-        start = pl.multiple_of(chunk * span, span)
-        relay.own(chunk, tokens.at[pl.ds(start, span), :])
+        relay.own(chunk, tokens.at[rows_of(chunk), :])
         return carry
 
     lax.fori_loop(0, count, begin, 0)
@@ -187,10 +204,10 @@
     load.wait()
 
     def to_frame(chunk, s):
-        start = pl.multiple_of(chunk * span, span)
-        return send(
-            kv_ref.at[0, :, pl.ds(start, span), :],
-            kv_ref.at[s, :, pl.ds(start, span), :],
+        window = rows_of(chunk)
+        return send(
+            kv_ref.at[0, :, window, :],
+            kv_ref.at[s, :, window, :],
             kv_send.at[chunk, s],
             kv_recv.at[chunk, s],
             frame=target_of(frame, frames, s),
@@ -203,7 +220,21 @@
             head=there,
         )
 
-    late = max(heads_axis // 2 - 2, 0)
+    def band_to(s):
+        return send(
+            band_ref, full.at[:, band, :], x_send.at[s], x_recv.at[s],
+            frame=target_of(frame, frames, s),
+        )
+
+    def band_from(s):
+        there = source_of(frame, frames, s)
+        part = pl.ds(pl.multiple_of(there * share, share), share)
+        return send(
+            full.at[:, part, :], full.at[:, part, :], x_send.at[s], x_recv.at[s],
+            frame=target_of(frame, frames, s),
+        )
+
+    late = max(line - 2, 0)
 
     def turn(i, carry):
         relay.advance(i, count)
@@ -221,8 +252,7 @@
 
     def step(chunk):
         relay.collect(chunk)
-        start = pl.multiple_of(chunk * span, span)
-        window = pl.ds(start, span)
+        window = rows_of(chunk)
         total = jnp.zeros((span, cols), jnp.float32)
         for i in range(heads_axis):
             total += got[i, window, :].astype(jnp.float32)
@@ -234,11 +264,11 @@
         inverse = lax.rsqrt(jnp.sum(square, axis=1, keepdims=True) / width + EPSILON)
         parts = []
         for i in range(heads_axis):
-            wide = got[i, window, :].astype(jnp.float32)
+            wide_part = got[i, window, :].astype(jnp.float32)
             shift = modulation[0:1, i * cols : (i + 1) * cols]
             gain = modulation[1:2, i * cols : (i + 1) * cols]
             parts.append(
-                ((wide - center) * inverse * (1.0 + gain) + shift).astype(jnp.bfloat16)
+                ((wide_part - center) * inverse * (1.0 + gain) + shift).astype(jnp.bfloat16)
             )
         sums = [contract(parts, held[j]) for j in range(3)]
         q_ref[window, :] = sums[0].astype(q_ref.dtype)
@@ -249,104 +279,16 @@
 
     lax.fori_loop(0, count + late, turn, 0)
 
-    def finish(chunk, carry):
-        relay.drain(chunk)
+    def arrive(chunk, carry):
         for s in range(1, frames):
-            to_frame(chunk, s).wait()
-        return carry
-
-    lax.fori_loop(0, count, finish, 0)
-    keep.wait()
-    for s in range(1, heads_axis):
-        there = source_of(me, heads_axis, s)
-        ref = band_ref.at[there]
-        send(ref, ref, w_send.at[s], w_recv.at[s], head=target_of(me, heads_axis, s)).wait_recv()
-        to_head(s).wait_send()
-
-
-def gather_project(frames, heads_axis, tokens, modulation, weight, out_weight):
-    rows, cols = tokens.shape
-    inner = weight.shape[2]
-    count = TOKEN_CHUNKS
-    line = heads_axis // 2
-    whole = pl.BlockSpec(memory_space=pltpu.VMEM)
-    away = pl.BlockSpec(memory_space=pl.ANY)
-    sem = pltpu.SemaphoreType.DMA
-    if cols % 128 == 0:
-        def w_slice(ref, band, there):
-            return ref.at[band, pl.ds(pl.multiple_of(there * cols, cols), cols)]
-    else:
-        out_weight = out_weight.reshape(inner, heads_axis, cols).transpose(1, 0, 2)
-
-        def w_slice(ref, band, there):
-            return ref.at[there, band, :]
-
-    return pl.pallas_call(
-        functools.partial(gather_kernel, frames, heads_axis, count, w_slice),
-        in_specs=[away, whole, away, away],
-        out_specs=[whole, whole, whole],
-        out_shape=[
-            jax.ShapeDtypeStruct((rows, inner), jnp.bfloat16),
-            jax.ShapeDtypeStruct((frames, 2, rows, inner), jnp.bfloat16),
-            jax.ShapeDtypeStruct((heads_axis, inner // frames, cols), jnp.bfloat16),
-        ],
-        scratch_shapes=[
-            pltpu.VMEM((heads_axis, rows, cols), jnp.bfloat16),
-            pltpu.VMEM(weight.shape, jnp.bfloat16),
-            sem((line, count, 2)),
-            sem((line, count)),
-            sem((line, count)),
-            sem((line, count)),
-            sem((count, frames)),
-            sem((count, frames)),
-            sem((heads_axis,)),
-            sem((heads_axis,)),
-            sem((3,)),
-        ],
-        compiler_params=pltpu.CompilerParams(collective_id=0, has_side_effects=True),
-        name="gather_project",
-    )(tokens, modulation, weight, out_weight)
-
-
-def attend_kernel(
-    frames, heads_axis, heads, count, q_ref, kv_ref, mask_ref, band_ref, tokens, gate,
-    out_ref, done, full, far_send, far_recv, pair_send, pair_recv, x_send, x_recv, local,
-):
-    me, frame = lax.axis_index("head"), lax.axis_index("frame")
-    rows, inner = q_ref.shape
-    head_size = inner // heads
-    factor = LOG2E / math.sqrt(head_size)
-    span = rows // count
-    share = inner // frames
-    greet(me, frame, heads_axis, frames)
-    relay = Relay(me, heads_axis, done, span, (far_send, far_recv, pair_send, pair_recv))
-    band = pl.ds(pl.multiple_of(frame * share, share), share)
-
-    keep = pltpu.make_async_copy(band_ref, full.at[:, band, :], local.at[0])
-    keep.start()
-
-    def to_frame(s):
-        return send(
-            band_ref, full.at[:, band, :], x_send.at[s], x_recv.at[s],
-            frame=target_of(frame, frames, s),
-        )
-
-    def from_frame(s):
-        there = source_of(frame, frames, s)
-        part = pl.ds(pl.multiple_of(there * share, share), share)
-        return send(
-            full.at[:, part, :], full.at[:, part, :], x_send.at[s], x_recv.at[s],
-            frame=target_of(frame, frames, s),
-        )
-
-    for s in range(1, frames):
-        to_frame(s).start()
+            to_frame(chunk, s).wait_recv()
+        return carry
+
+    lax.fori_loop(0, count, arrive, 0)
     sources = [source_of(frame, frames, s) * (rows // BLK) for s in range(frames)]
 
-    wide = span // BLK
-
     def tile(t, carry):
-        window = pl.ds(pl.multiple_of(t * span, span), span)
+        window = rows_of(t)
         for h in range(heads):
             lanes = slice(h * head_size, (h + 1) * head_size)
             query = q_ref[window, lanes]
@@ -392,97 +334,135 @@
                 top = new_top
             done[me, window, lanes] = (summed / total).T.astype(done.dtype)
 
-        relay.own(t)
-
-        @pl.when(t >= 1)
-        def _():
-            relay.advance(t - 1, count)
+        spread.own(t)
+
+        @pl.when(jnp.logical_and(inside, t >= 1))
+        def _():
+            spread.pass_all(t - 1, False)
 
         return carry
 
     lax.fori_loop(0, count, tile, 0)
 
-    late = max(heads_axis // 2 - 2, 0)
-
-    def rest(i, carry):
-        relay.advance(i, count)
-        return carry
-
-    lax.fori_loop(count - 1, count + late - 1, rest, 0)
     keep.wait()
+    for s in range(1, heads_axis):
+        there = source_of(me, heads_axis, s)
+        ref = band_ref.at[there]
+        send(ref, ref, w_send.at[s], w_recv.at[s], head=target_of(me, heads_axis, s)).wait_recv()
+    lay = pltpu.make_async_copy(band_ref, full.at[:, band, :], local.at[3])
+    lay.start()
     for s in range(1, frames):
-        from_frame(s).wait_recv()
-
-    def out(t, carry):
-        @pl.when(t == count - 1)
-        def _():
-            relay.advance(count + late - 1, count)
-
-        relay.collect(t)
-        window = pl.ds(pl.multiple_of(t * span, span), span)
-        weight = full[...].reshape(heads_axis * inner, full.shape[2])
-        total = contract([done[i, window, :] for i in range(heads_axis)], weight)
+        band_to(s).start()
+
+    def near(t, carry):
+        spread.pass_all(t, False)
+        return carry
+
+    lax.fori_loop(jnp.where(inside, count - 1, 0), count, near, 0)
+    lay.wait()
+
+    def out(t):
+        spread.collect(t)
+        window = rows_of(t)
+        plane = full[...].reshape(heads_axis * inner, full.shape[2])
+        total = contract([done[i, window, :] for i in range(heads_axis)], plane)
         if gate.shape[1] == out_ref.shape[1]:
             own = gate[...]
         else:
-            cols = out_ref.shape[1]
             own = gate[2:3, pl.ds(pl.multiple_of(me * cols, cols), cols)]
-        held = tokens[window, :].astype(jnp.float32)
-        out_ref[window, :] = (held + own * total).astype(out_ref.dtype)
-        return carry
-
-    lax.fori_loop(0, count, out, 0)
-
-    def finish(t, carry):
-        relay.drain(t)
+        wide_part = got[me, window, :].astype(jnp.float32)
+        out_ref[window, :] = (wide_part + own * total).astype(out_ref.dtype)
+
+    def last(t, carry):
+        @pl.when(t < count)
+        def _():
+            spread.pass_all(t, True)
+
+        @pl.when(t == 0)
+        def _():
+            for s in range(1, frames):
+                band_from(s).wait_recv()
+
+        @pl.when(t >= 1)
+        def _():
+            out(t - 1)
+
+        return carry
+
+    lax.fori_loop(0, count + 1, last, 0)
+
+    def finish(chunk, carry):
+        relay.drain(chunk)
+        spread.drain(chunk)
+        for s in range(1, frames):
+            to_frame(chunk, s).wait_send()
         return carry
 
     lax.fori_loop(0, count, finish, 0)
+    for s in range(1, heads_axis):
+        to_head(s).wait_send()
     for s in range(1, frames):
-        to_frame(s).wait_send()
-
-
-def attend_mix(frames, heads_axis, heads, query, pairs, mask, band, tokens, gate):
-    rows, inner = query.shape
-    cols = tokens.shape[1]
-    count = QUERY_CHUNKS
+        band_to(s).wait_send()
+
+
+def sublayer(frames, heads_axis, heads, tokens, modulation, weight, out_weight, mask, gate):
+    rows, cols = tokens.shape
+    inner = weight.shape[2]
+    count = CHUNKS
     line = heads_axis // 2
     whole = pl.BlockSpec(memory_space=pltpu.VMEM)
     away = pl.BlockSpec(memory_space=pl.ANY)
     sem = pltpu.SemaphoreType.DMA
+    if cols % 128 == 0:
+        def w_slice(ref, band, there):
+            return ref.at[band, pl.ds(pl.multiple_of(there * cols, cols), cols)]
+    else:
+        out_weight = out_weight.reshape(inner, heads_axis, cols).transpose(1, 0, 2)
+
+        def w_slice(ref, band, there):
+            return ref.at[there, band, :]
+
+    relay_sems = [sem((line, count, 2)), sem((line, count)), sem((line, count)), sem((line, count))]
     return pl.pallas_call(
-        functools.partial(attend_kernel, frames, heads_axis, heads, count),
-        in_specs=[whole, whole, pl.BlockSpec(memory_space=pltpu.SMEM), whole, whole, whole],
+        functools.partial(block_kernel, frames, heads_axis, heads, count, w_slice),
+        in_specs=[
+            away, whole, away, away, pl.BlockSpec(memory_space=pltpu.SMEM), whole,
+        ],
         out_specs=whole,
         out_shape=jax.ShapeDtypeStruct((rows, cols), jnp.bfloat16),
         scratch_shapes=[
+            pltpu.VMEM((heads_axis, rows, cols), jnp.bfloat16),
+            pltpu.VMEM(weight.shape, jnp.bfloat16),
+            pltpu.VMEM((rows, inner), jnp.bfloat16),
+            pltpu.VMEM((frames, 2, rows, inner), jnp.bfloat16),
+            pltpu.VMEM((heads_axis, inner // frames, cols), jnp.bfloat16),
+            pltpu.VMEM((heads_axis, inner, cols), jnp.bfloat16),
             pltpu.VMEM((heads_axis, rows, inner), jnp.bfloat16),
-            pltpu.VMEM((heads_axis, inner, cols), jnp.bfloat16),
-            sem((line, count, 2)),
-            sem((line, count)),
-            sem((line, count)),
-            sem((line, count)),
+            *relay_sems,
+            *relay_sems,
+            sem((count, frames)),
+            sem((count, frames)),
+            sem((heads_axis,)),
+            sem((heads_axis,)),
             sem((frames,)),
             sem((frames,)),
-            sem((1,)),
+            sem((4,)),
         ],
-        compiler_params=pltpu.CompilerParams(collective_id=1, has_side_effects=True),
-        name="attend_mix",
-    )(query, pairs, mask, band, tokens, gate)
+        compiler_params=pltpu.CompilerParams(collective_id=0, has_side_effects=True),
+        name="sublayer",
+    )(tokens, modulation, weight, out_weight, mask, gate)
 
 
 def shards(frames, heads_axis, tokens, qkv_weight, out_weight, modulation, block_mask):
-    local_rows, local_cols = tokens.shape
-    heads_here = block_mask.shape[0]
-    head = lax.axis_index("head")
+    local_cols = tokens.shape[1]
     gate = modulation
     if local_cols % 128:
+        head = lax.axis_index("head")
         gate = lax.dynamic_slice_in_dim(modulation[2:3], head * local_cols, local_cols, 1)
-
-    query, pairs, band = gather_project(
-        frames, heads_axis, tokens, modulation, qkv_weight, out_weight
+    return sublayer(
+        frames, heads_axis, block_mask.shape[0], tokens, modulation, qkv_weight, out_weight,
+        block_mask, gate,
     )
-    return attend_mix(frames, heads_axis, heads_here, query, pairs, block_mask, band, tokens, gate)
 
 
 def solution(mesh):

time: 167 us -> 187 us (1.12)
  Pallas kernels: 165 us -> 184 us
    pallas_call x2 -> x1, Pallas kernels: 165 us -> 184 us  [sublayer(): pl.pallas_call(functools.partial(block_kernel, frames, heads_axis, heads,...]
where the time goes in v1:
time: 187 us; the launch traced here: 186 us
  Pallas kernels  184 us (98%)
  local copies, waits for them, and re-layouts  2.49 us (1%)
    pallas_call x1, Pallas kernels, sublayer(): pl.pallas_call(functools.partial(block_kernel, frames, heads_axis, heads,...  184 us

profile of v1, /device:TPU:1, one launch (start us, length us, event | category | flops | bytes accessed | tf_op | source)
XLA Modules:
  0.0 186.4 jit_solution(11165767912645192496)
XLA Ops:
  0.0 183.9 %sublayer.1 = bf16[1024,640]{1,0:T(8,128)(2,1)} custom-call(bf16[1024,640]{1,0:T(8,128)(2,1)} %tokens.1, f32[3,5120]{1,0:T(4,128)} %gate.1, bf16[3,5120,256]{2,1,0:T(8,128)(2,1)} %weight.1, bf16[256,5120]{1,0:T(8,128)(2,1)} %out_weight.1, s32[2,8,32]{2,1,0:T(8,128)} %mask_ref.1, f32[3,5120]{1,0:T(4,128)} %gate.1), custom_call_target="tpu_custom_call" | custom-call | tf_op jit(solution)/shard_map/sublayer/pallas_call | solution.py:426
  183.9 2.5 %copy.7 = bf16[1024,640]{1,0:T(8,128)(2,1)} copy(bf16[1024,640]{1,0:T(8,128)(2,1)} %sublayer.1) | data formatting | bytes 2621440

commit v2 on v1

--- a/solution.py
+++ b/solution.py
@@ -13,6 +13,7 @@
 EPSILON = 1e-06
 LOG2E = math.log2(math.e)
 CHUNKS = 8
+AHEAD = 2
 
 
 def source_of(me, size, step):
@@ -104,13 +105,13 @@
 
                 self.pair(block, chunk).start()
 
-    def advance(self, turn, count):
+    def advance(self, turn, count, ends=None):
         for distance in range(1, self.line):
             chunk = turn - (distance - 1)
 
             @pl.when(jnp.logical_and(chunk >= 0, chunk < count))
             def _():
-                self.pass_on(chunk, distance)
+                self.pass_on(chunk, distance, ends)
 
     def pass_all(self, chunk, ends):
         for distance in range(1, self.line):
@@ -199,10 +200,6 @@
         relay.own(chunk, tokens.at[rows_of(chunk), :])
         return carry
 
-    lax.fori_loop(0, count, begin, 0)
-    mine.wait()
-    load.wait()
-
     def to_frame(chunk, s):
         window = rows_of(chunk)
         return send(
@@ -220,6 +217,14 @@
             head=there,
         )
 
+    def band_in(s):
+        ref = band_ref.at[source_of(me, heads_axis, s)]
+        return send(
+            ref, ref, w_send.at[s], w_recv.at[s], head=target_of(me, heads_axis, s)
+        )
+
+    lay = pltpu.make_async_copy(band_ref, full.at[:, band, :], local.at[3])
+
     def band_to(s):
         return send(
             band_ref, full.at[:, band, :], x_send.at[s], x_recv.at[s],
@@ -235,14 +240,27 @@
         )
 
     late = max(line - 2, 0)
+    for s in range(1, heads_axis):
+        to_head(s).start()
+    lax.fori_loop(0, AHEAD, begin, 0)
+    mine.wait()
+    load.wait()
 
     def turn(i, carry):
+        @pl.when(i + AHEAD < count)
+        def _():
+            begin(i + AHEAD, 0)
+
+        @pl.when(i == 1)
+        def _():
+            keep.wait()
+            for s in range(1, heads_axis):
+                band_in(s).wait_recv()
+            lay.start()
+            for s in range(1, frames):
+                band_to(s).start()
+
         relay.advance(i, count)
-
-        @pl.when(i == count + late - 2)
-        def _():
-            for s in range(1, heads_axis):
-                to_head(s).start()
 
         @pl.when(i >= late)
         def _():
@@ -344,16 +362,6 @@
 
     lax.fori_loop(0, count, tile, 0)
 
-    keep.wait()
-    for s in range(1, heads_axis):
-        there = source_of(me, heads_axis, s)
-        ref = band_ref.at[there]
-        send(ref, ref, w_send.at[s], w_recv.at[s], head=target_of(me, heads_axis, s)).wait_recv()
-    lay = pltpu.make_async_copy(band_ref, full.at[:, band, :], local.at[3])
-    lay.start()
-    for s in range(1, frames):
-        band_to(s).start()
-
     def near(t, carry):
         spread.pass_all(t, False)
         return carry
@@ -373,23 +381,21 @@
         wide_part = got[me, window, :].astype(jnp.float32)
         out_ref[window, :] = (wide_part + own * total).astype(out_ref.dtype)
 
-    def last(t, carry):
-        @pl.when(t < count)
+    for s in range(1, frames):
+        band_from(s).wait_recv()
+
+    behind = line - 1
+
+    def last(i, carry):
+        spread.advance(i, count, True)
+
+        @pl.when(i >= behind)
         def _():
-            spread.pass_all(t, True)
-
-        @pl.when(t == 0)
-        def _():
-            for s in range(1, frames):
-                band_from(s).wait_recv()
-
-        @pl.when(t >= 1)
-        def _():
-            out(t - 1)
-
-        return carry
-
-    lax.fori_loop(0, count + 1, last, 0)
+            out(i - behind)
+
+        return carry
+
+    lax.fori_loop(0, count + behind, last, 0)
 
     def finish(chunk, carry):
         relay.drain(chunk)

time: 187 us -> 155 us (0.83)
  Pallas kernels: 184 us -> 153 us
    pallas_call x1, Pallas kernels: 184 us -> 153 us  [sublayer(): pl.pallas_call(functools.partial(block_kernel, frames, heads_axis, heads,...]
where the time goes in v2:
time: 155 us
  Pallas kernels  153 us (99%)
  local copies, waits for them, and re-layouts  2.49 us (2%)
    pallas_call x1, Pallas kernels, sublayer(): pl.pallas_call(functools.partial(block_kernel, frames, heads_axis, heads,...  153 us

profile of v2, /device:TPU:1, one launch (start us, length us, event | category | flops | bytes accessed | tf_op | source)
XLA Modules:
  0.0 155.1 jit_solution(9495496015555752512)
XLA Ops:
  0.0 152.6 %sublayer.1 = bf16[1024,640]{1,0:T(8,128)(2,1)} custom-call(bf16[1024,640]{1,0:T(8,128)(2,1)} %tokens.1, f32[3,5120]{1,0:T(4,128)} %gate.1, bf16[3,5120,256]{2,1,0:T(8,128)(2,1)} %weight.1, bf16[256,5120]{1,0:T(8,128)(2,1)} %out_weight.1, s32[2,8,32]{2,1,0:T(8,128)} %mask_ref.1, f32[3,5120]{1,0:T(4,128)} %gate.1), custom_call_target="tpu_custom_call" | custom-call | tf_op jit(solution)/shard_map/sublayer/pallas_call | solution.py:432
  152.7 2.5 %copy.7 = bf16[1024,640]{1,0:T(8,128)(2,1)} copy(bf16[1024,640]{1,0:T(8,128)(2,1)} %sublayer.1) | data formatting | bytes 2621440
